TPU v7x, 128 devices: a whole 4x4x4 slice. The times are simulated.
128 devices in a mesh: tm: 8 (over y, x_hi), agent: 16 (over z, x_lo, core).
Axes of the slice: x: 4 (x_hi: 2, x_lo: 2; x = x_hi * 2 + x_lo), y: 4, z: 4, core: 2. Of those that a mesh axis runs over, the one named last changes fastest.
Arguments:
- tokens: bfloat16 [32, 1024, 1024], P('tm', 'agent'), may hold values from -6 to 6
- conv_taps: float32 [5, 1024], replicated, may hold values from -3 to 3
- norm_first: float32 [1024], replicated, may hold values from 0.1 to 1.9
- norm_second: float32 [1024], replicated, may hold values from 0.1 to 1.9
- norm_third: float32 [1024], replicated, may hold values from 0.1 to 1.9
- w_in: bfloat16 [1024, 3072], replicated, may hold values from -0.1875 to 0.1875
- w_out: bfloat16 [3072, 1024], replicated, may hold values from -0.109375 to 0.109375
- w_query: bfloat16 [1024, 1024], replicated, may hold values from -16 to 16
- w_key: bfloat16 [1024, 1024], replicated, may hold values from -16 to 16
- w_value: bfloat16 [1024, 1024], replicated, may hold values from -0.1875 to 0.1875
- w_output: bfloat16 [1024, 1024], replicated, may hold values from -0.1875 to 0.1875
- agent_order: int32 [1024], P('agent'), may hold values from 0 to 1023, each once
- present_steps: int32 [1024], P('agent'), may hold values from 1 to 32
Outputs:
- result: bfloat16 [32, 1024, 1024], P('tm', 'agent')
Inputs may be any that keep to these rules, and one draw needn't show every extreme that they name: `agent_order`: each of 0 to 1023 appears once.
All inputs are finite; a program needn't handle non-finite values.
Results may differ from a plain program's by a relative error of at most 0.012.
Values may be sent and summed in bfloat16 or wider, within the bound.
A program may use at most 192 MiB of HBM per device.

v0:
```python
import jax
import jax.numpy as jnp
from jax import lax
from jax.sharding import PartitionSpec as P

HEADS = 16
EPS = 1e-05


def shifted(shard, axis, by):
    count = lax.axis_size(axis)
    pairs = [(i, i + by) for i in range(count) if 0 <= i + by < count]
    return lax.ppermute(shard, axis, pairs)


def normed_rows(rows, gain):
    values = rows.astype(jnp.float32)
    scale = lax.rsqrt(jnp.mean(values * values, axis=-1, keepdims=True) + EPS)
    return values * scale * gain


def make_absorb(query, own_order, steps, heads_here, project):
    step_count, agent_count, width = query.shape
    head_size = width // heads_here
    scale = head_size ** (-0.5)
    split_query = query.reshape(step_count, agent_count, heads_here, head_size)
    init = (
        jnp.full((step_count, heads_here, agent_count), -1e30, jnp.float32),
        jnp.zeros((step_count, heads_here, agent_count), jnp.float32),
        jnp.zeros((step_count, agent_count, heads_here, head_size), jnp.float32),
    )

    def absorb(carry, piece, start):
        best, total, summed = carry
        key_piece, value_piece, order_piece, present_piece = project(piece)
        count = key_piece.shape[1]
        key_piece = key_piece.reshape(step_count, count, heads_here, head_size)
        value_piece = value_piece.reshape(step_count, count, heads_here, head_size)
        scores = (
            jnp.einsum(
                "sahd,sbhd->shab", split_query, key_piece, preferred_element_type=jnp.float32
            )
            * scale
        )
        other_order = order_piece[0]
        earlier = other_order[None, None, :] < own_order[None, :, None]
        alive = steps[:, None, None] < present_piece[0][None, None, :]
        itself = other_order[None, None, :] == own_order[None, :, None]
        visible = (earlier & alive | itself)[:, None]
        masked = jnp.where(visible, scores, -1e30)
        fresh = jnp.maximum(best, jnp.max(masked, axis=-1))
        weights = jnp.where(visible, jnp.exp(masked - fresh[..., None]), 0.0).astype(jnp.bfloat16)
        total = jnp.sum(weights.astype(jnp.float32), axis=-1)
        part_sum = jnp.einsum(
            "shab,sbhd->sahd", weights, value_piece, preferred_element_type=jnp.float32
        )
        summed = part_sum
        return (fresh, total, summed)

    return (absorb, init)


def finish(carry, shape):
    best, total, summed = carry
    attended = summed / jnp.transpose(total, (0, 2, 1))[..., None]
    return attended.astype(jnp.bfloat16).reshape(shape)


def identity_piece(piece):
    return piece


def per_device(
    tokens,
    conv_taps,
    norm_first,
    norm_second,
    norm_third,
    w_in,
    w_out,
    w_query,
    w_key,
    w_value,
    w_output,
    agent_order,
    present_steps,
):
    step_count, agent_count, width = tokens.shape
    reach = conv_taps.shape[0] - 1
    earlier_steps = shifted(tokens, "tm", 1)
    extended = normed_rows(jnp.concatenate([earlier_steps, tokens], axis=0), norm_first)
    mixed = jnp.zeros((step_count, agent_count, width), jnp.float32)
    for lag in range(reach + 1):
        mixed = mixed + conv_taps[lag] * extended[reach - lag : reach - lag + step_count]
    first = (tokens.astype(jnp.float32) + mixed).astype(jnp.bfloat16)
    flat = first.reshape(step_count * agent_count, width)
    inner = normed_rows(flat, norm_second).astype(jnp.bfloat16)
    hidden = jax.nn.gelu(
        jnp.dot(inner, w_in, preferred_element_type=jnp.float32), approximate=False
    ).astype(jnp.bfloat16)
    second = (
        flat.astype(jnp.float32) + jnp.dot(hidden, w_out, preferred_element_type=jnp.float32)
    ).astype(jnp.bfloat16)
    attn_in = normed_rows(second, norm_third).astype(jnp.bfloat16)
    query = (
        jnp.dot(attn_in, w_query, preferred_element_type=jnp.float32)
        .astype(jnp.bfloat16)
        .reshape(step_count, agent_count, width)
    )
    order_rows = agent_order.reshape(1, agent_count)
    present_rows = present_steps.reshape(1, agent_count)
    keys = (
        jnp.dot(attn_in, w_key, preferred_element_type=jnp.float32)
        .astype(jnp.bfloat16)
        .reshape(step_count, agent_count, width)
    )
    values = (
        jnp.dot(attn_in, w_value, preferred_element_type=jnp.float32)
        .astype(jnp.bfloat16)
        .reshape(step_count, agent_count, width)
    )
    keys, values = (keys, values)
    query, keys, values = (
        lax.all_to_all(query, "tm", split_axis=2, concat_axis=0, tiled=True),
        lax.all_to_all(keys, "tm", split_axis=2, concat_axis=0, tiled=True),
        lax.all_to_all(values, "tm", split_axis=2, concat_axis=0, tiled=True),
    )
    steps = jnp.arange(query.shape[0], dtype=jnp.int32)
    heads_here = HEADS // lax.axis_size("tm")
    absorb, init = make_absorb(query, agent_order, steps, heads_here, identity_piece)
    carry = absorb(
        init,
        (
            lax.all_gather(keys, "agent", axis=1, tiled=True),
            lax.all_gather(values, "agent", axis=1, tiled=True),
            lax.all_gather(order_rows, "agent", axis=1, tiled=True),
            lax.all_gather(present_rows, "agent", axis=1, tiled=True),
        ),
        jnp.int32(0),
    )
    attended = finish(carry, query.shape)
    attended = lax.all_to_all(attended, "tm", split_axis=0, concat_axis=2, tiled=True)
    projected = jnp.dot(
        attended.reshape(step_count * agent_count, width),
        w_output,
        preferred_element_type=jnp.float32,
    )
    result = second.astype(jnp.float32) + projected
    return result.astype(jnp.bfloat16).reshape(step_count, agent_count, width)


def solution(mesh):
    in_specs = (
        P("tm", "agent", None),
        P(),
        P(),
        P(),
        P(),
        P(),
        P(),
        P(),
        P(),
        P(),
        P(),
        P("agent"),
        P("agent"),
    )
    out_specs = P("tm", "agent", None)
    return jax.shard_map(
        per_device, mesh=mesh, in_specs=in_specs, out_specs=out_specs, check_vma=False
    )
```

profile of v0, /device:TPU:0, one launch (start us, length us, event | category | flops | bytes accessed | tf_op | source)
XLA Modules:
  0.0 235.1 jit_solution(14129081017646608805)
XLA Ops:
  6.5 5.3 %collective-permute-start = (bf16[4,64,1024]{2,1,0:T(8,128)(2,1)}, bf16[4,64,1024]{2,1,0:T(8,128)(2,1)S(1)}, u32[]{:S(2)}, u32[]{:S(2)}) collective-permute-start(bf16[4,64,1024]{2,1,0:T(8,128)(2,1)} %param.13), channel_id=1, source_target_pairs={{0,16},{16,32},{32,48},{48,64},{64,80},{80,96},{96,112},{1,17},{17... | collective-permute-start | bytes 1572872 | tf_op jit(solution)/shard_map/ppermute | solution.py:13
  12.8 10.5 %collective-permute-done = bf16[4,64,1024]{2,1,0:T(8,128)(2,1)S(1)} collective-permute-done((bf16[4,64,1024]{2,1,0:T(8,128)(2,1)}, bf16[4,64,1024]{2,1,0:T(8,128)(2,1)S(1)}, u32[]{:S(2)}, u32[]{:S(2)}) %collective-permute-start) | collective-permute-done | bytes 524320 | tf_op jit(solution)/shard_map/ppermute | solution.py:13
  26.9 15.0 %fusion.53 = (f32[256]{0:T(256)S(1)}, bf16[256,1024]{1,0:T(8,128)(2,1)}) fusion(bf16[3072,1024]{1,0:T(8,128)(2,1)} %param.19, bf16[256,1024]{1,0:T(8,128)(2,1)S(1)} %fusion.63, bf16[1024,3072]{1,0:T(8,128)(2,1)} %param.18, bf16[256,1024]{1,0:T(8,128)(2,1)S(1)} %bitcast.69), kind=kOutput, calls=%fused_computation.70 | convolution fusion | flops 3273916160 | bytes 14156800 | tf_op jit(solution)/shard_map/dot_general | solution.py:102
  41.9 1.8 convolution_convert_fusion
  45.4 18.3 %all_to_all.66 = bf16[8,2,16384]{2,1,0:T(2,128)(2,1)S(1)} all-to-all(bf16[8,2,16384]{2,1,0:T(2,128)(2,1)S(1)} %reshape.197), channel_id=1, replica_groups=mesh['tm'=8,'agent'=16] {'tm'}, dimensions={0} | all-to-all | bytes 1048576 | tf_op jit(solution)/shard_map/all_to_all | solution.py:125
  65.8 2.4 %convolution_convert_fusion.2 = bf16[256,1024]{1,0:T(8,128)(2,1)S(1)} fusion(bf16[1024,1024]{1,0:T(8,128)(2,1)} %param.22, bf16[256,1024]{1,0:T(8,128)(2,1)S(1)} %copy-done.8, f32[1024]{0:T(1024)S(1)} %copy-done.5, f32[256]{0:T(256)S(1)} %add_rsqrt_fusion.2), kind=kOutput, calls=%fused_computation.68 | convolution fusion | flops 538181632 | bytes 3150848 | tf_op jit(solution)/shard_map/dot_general | solution.py:118
  69.6 17.9 %all_to_all.67 = bf16[8,2,16384]{2,1,0:T(2,128)(2,1)S(1)} all-to-all(bf16[8,2,16384]{2,1,0:T(2,128)(2,1)S(1)} %reshape.195), channel_id=1, replica_groups=mesh['tm'=8,'agent'=16] {'tm'}, dimensions={0} | all-to-all | bytes 1048576 | tf_op jit(solution)/shard_map/all_to_all | solution.py:126
  91.4 14.2 %all-reduce.2 = (s32[1024]{0:T(1024)S(1)}, s32[1024]{0:T(1024)S(1)}) all-reduce(s32[1024]{0:T(1024)S(1)} %dynamic-update-slice, s32[1024]{0:T(1024)S(1)} %dynamic-update-slice.1), channel_id=2, replica_groups=mesh['tm'=8,'agent'=16] {'agent'}, use_global_device_ids=true, to_apply=%add | all-reduce | flops 2048 | bytes 16384
  105.9 2.4 %convolution_convert_fusion.1 = bf16[256,1024]{1,0:T(8,128)(2,1)S(1)} fusion(bf16[1024,1024]{1,0:T(8,128)(2,1)} %param.20, bf16[256,1024]{1,0:T(8,128)(2,1)S(1)} %copy-done.8, f32[1024]{0:T(1024)S(1)} %copy-done.5, f32[256]{0:T(256)S(1)} %add_rsqrt_fusion.2), kind=kOutput, calls=%fused_computation.67 | convolution fusion | flops 538181632 | bytes 3150848 | tf_op jit(solution)/shard_map/dot_general | solution.py:106
  109.0 1.5 reshape.199
  110.5 4.4 %all-to-all-start.1 = ((bf16[8,2,16384]{2,1,0:T(2,128)(2,1)}), bf16[8,2,16384]{2,1,0:T(2,128)(2,1)}, u32[]{:S(2)}, u32[]{:S(2)}) async-start(bf16[8,2,16384]{2,1,0:T(2,128)(2,1)} %reshape.199), calls=%async_computation.1 | async-start | bytes 1048576 | tf_op jit(solution)/shard_map/all_to_all | solution.py:124
  114.9 1.4 and_or_fusion
  116.3 10.8 %all-to-all-done.1 = bf16[8,2,16384]{2,1,0:T(2,128)(2,1)} async-done(((bf16[8,2,16384]{2,1,0:T(2,128)(2,1)}), bf16[8,2,16384]{2,1,0:T(2,128)(2,1)}, u32[]{:S(2)}, u32[]{:S(2)}) %all-to-all-start.1) | async-done | bytes 524320 | tf_op jit(solution)/shard_map/all_to_all | solution.py:124
  127.1 2.7 %reshape.200 = bf16[1024,4,64]{2,1,0:T(4,128)(2,1)S(1)} reshape(bf16[8,2,16384]{2,1,0:T(2,128)(2,1)} %all-to-all-done.1) | data formatting | bytes 1048576
  131.0 2.4 %reshape.174 = bf16[32,64,2,64]{3,2,1,0:T(2,128)(2,1)S(1)} reshape(bf16[8,4,64,128]{3,2,1,0:T(8,128)(2,1)} %bitcast.70) | data formatting | bytes 1048576 | tf_op jit(solution)/shard_map/reshape | solution.py:26
  133.5 12.5 %copy.33 = bf16[32,1024,128]{1,2,0:T(8,128)(2,1)} copy(bf16[32,1024,128]{2,0,1:T(8,128)(2,1)} %all-gather.7.cloned.1.call-done) | data formatting | bytes 16777216 | tf_op jit(solution)/shard_map/all_gather | solution.py:134
  146.0 10.3 %fusion = (f32[32,2,64]{2,1,0:T(2,128)S(1)}, f32[32,2,64,1024]{3,2,1,0:T(8,128)}) fusion(pred[32,64,1024]{2,1,0:T(8,128)(4,1)S(1)} %and_or_fusion, bf16[32,1024,2,64]{1,3,2,0:T(8,128)(2,1)} %bitcast.61, bf16[32,64,2,64]{3,2,1,0:T(2,128)(2,1)S(1)} %reshape.174), kind=kOutput, calls=%fused_computation.3 | convolution fusion | flops 549449728 | bytes 27803648 | tf_op jit(solution)/shard_map/sahd,sbhd->shab/dot_general | solution.py:40
  156.3 9.0 %convert_reduce_fusion = f32[32,2,64]{2,1,0:T(2,128)S(1)} fusion(f32[32,2,64]{2,1,0:T(2,128)S(1)} %broadcast_maximum_fusion, f32[32,2,64,1024]{3,2,1,0:T(8,128)} %get-tuple-element.19, pred[32,64,1024]{2,1,0:T(8,128)(4,1)S(1)} %and_or_fusion), kind=kLoop, calls=%fused_computation | loop fusion | flops 29356032 | bytes 18907136 | tf_op jit(solution)/shard_map/reduce_sum | solution.py:53
  165.3 15.4 %all-gather.5.cloned.1.call-done = bf16[32,1024,128]{2,0,1:T(8,128)(2,1)} async-done(((bf16[32,64,128]{2,0,1:T(8,128)(2,1)}), bf16[32,1024,128]{2,0,1:T(8,128)(2,1)}) %all-gather.5.cloned.1.call-update) | async-done | bytes 8388624 | tf_op jit(solution)/shard_map/all_gather | solution.py:135
  180.7 12.2 %copy.27 = bf16[32,1024,128]{1,2,0:T(8,128)(2,1)} copy(bf16[32,1024,128]{2,0,1:T(8,128)(2,1)} %all-gather.5.cloned.1.call-done) | data formatting | bytes 16777216 | tf_op jit(solution)/shard_map/all_gather | solution.py:135
  192.9 11.7 %fusion.13 = bf16[32,64,2,64]{1,3,2,0:T(8,128)(2,1)} fusion(bf16[32,1024,2,64]{1,3,2,0:T(8,128)(2,1)} %bitcast.62, f32[32,64,2]{1,2,0:T(2,128)S(1)} %bitcast.79, f32[32,2,64,1024]{3,2,1,0:T(8,128)} %get-tuple-element.19, f32[32,2,64]{2,1,0:T(2,128)S(1)} %broadcast_maximum_fusion, pred[32,64,1024]{2,1,0:T(8,128)(4,1)S(1)} %and_or_fusion), kind=kOutput, calls=%fused_computation.29 | convolution fusion | flops 558366720 | bytes 27820032 | tf_op jit(solution)/shard_map/shab,sbhd->sahd/dot_general | solution.py:54
  204.6 1.7 copy.35
  206.3 18.5 %all_to_all.68 = bf16[32,64,128]{2,1,0:T(8,128)(2,1)S(1)} all-to-all(bf16[32,64,128]{2,1,0:T(8,128)(2,1)S(1)} %copy.35), channel_id=1, replica_groups=mesh['tm'=8,'agent'=16] {'tm'}, dimensions={0} | all-to-all | bytes 1048576 | tf_op jit(solution)/shard_map/all_to_all | solution.py:142
  225.2 3.1 %fusion.49 = bf16[256,1024]{1,0:T(8,128)(2,1)} fusion(bf16[1024,1024]{1,0:T(8,128)(2,1)} %param.23, bf16[256,1024]{1,0:T(8,128)(2,1)S(1)} %copy-done.9, bf16[32,8,8,128]{3,2,1,0:T(8,128)(2,1)S(1)} %bitcast.78), kind=kOutput, calls=%fused_computation.65 | convolution fusion | flops 537657344 | bytes 3670016 | tf_op jit(solution)/shard_map/dot_general | solution.py:143
  (53 shorter events, 15.3 us)
Async XLA Ops:
  6.5 35.4 %copy-start = (bf16[1024,1024]{1,0:T(8,128)(2,1)S(1)}, bf16[1024,1024]{1,0:T(8,128)(2,1)}, u32[]{:S(2)}) copy-start(bf16[1024,1024]{1,0:T(8,128)(2,1)} %param.21) | copy-start | bytes 6291460
  6.5 19.4 %copy-start.2 = (bf16[4,64,1024]{2,1,0:T(8,128)(2,1)S(1)}, bf16[4,64,1024]{2,1,0:T(8,128)(2,1)}, u32[]{:S(2)}) copy-start(bf16[4,64,1024]{2,1,0:T(8,128)(2,1)} %param.13) | copy-start | bytes 1572868
  6.5 127.0 %all-gather.7.cloned.1.call-start = ((), (), s32[]{:S(2)}) async-start(), calls=%async_computation.5 | async-start | bytes 8912896 | tf_op jit(solution)/shard_map/all_gather | solution.py:134
  6.5 16.8 %collective-permute-start = (bf16[4,64,1024]{2,1,0:T(8,128)(2,1)}, bf16[4,64,1024]{2,1,0:T(8,128)(2,1)S(1)}, u32[]{:S(2)}, u32[]{:S(2)}) collective-permute-start(bf16[4,64,1024]{2,1,0:T(8,128)(2,1)} %param.13), channel_id=1, source_target_pairs={{0,16},{16,32},{32,48},{48,64},{64,80},{80,96},{96,112},{1,17},{17... | collective-permute-start | bytes 1572872 | tf_op jit(solution)/shard_map/ppermute | solution.py:13
  26.0 0.7 copy-start.3
  26.9 15.1 %copy-start.5 = (f32[1024]{0:T(1024)S(1)}, f32[1024]{0:T(1024)}, u32[]{:S(2)}) copy-start(f32[1024]{0:T(1024)} %param.17) | copy-start | bytes 12292
  44.6 21.1 %copy-start.8 = (bf16[256,1024]{1,0:T(8,128)(2,1)S(1)}, bf16[256,1024]{1,0:T(8,128)(2,1)}, u32[]{:S(2)}) copy-start(bf16[256,1024]{1,0:T(8,128)(2,1)} %get-tuple-element.17) | copy-start | bytes 1572868
  65.7 114.9 %all-gather.5.cloned.1.call-start = ((), (), s32[]{:S(2)}) async-start(), calls=%async_computation.4 | async-start | bytes 8912896 | tf_op jit(solution)/shard_map/all_gather | solution.py:135
  68.9 20.7 %copy-start.7 = (u32[128]{0:T(128)S(1)}, u32[128]{0:T(128)}, u32[]{:S(2)}) copy-start(u32[128]{0:T(128)} %constant.80) | copy-start | bytes 1540
  68.9 22.1 %copy-start.4 = (s32[64]{0:T(128)S(1)}, s32[64]{0:T(128)}, u32[]{:S(2)}) copy-start(s32[64]{0:T(128)} %param.24) | copy-start | bytes 772
  68.9 22.3 %copy-start.6 = (s32[64]{0:T(128)S(1)}, s32[64]{0:T(128)}, u32[]{:S(2)}) copy-start(s32[64]{0:T(128)} %param.25) | copy-start | bytes 772
  110.5 16.5 %all-to-all-start.1 = ((bf16[8,2,16384]{2,1,0:T(2,128)(2,1)}), bf16[8,2,16384]{2,1,0:T(2,128)(2,1)}, u32[]{:S(2)}, u32[]{:S(2)}) async-start(bf16[8,2,16384]{2,1,0:T(2,128)(2,1)} %reshape.199), calls=%async_computation.1 | async-start | bytes 1048576 | tf_op jit(solution)/shard_map/all_to_all | solution.py:124
  204.6 20.6 %copy-start.9 = (bf16[256,1024]{1,0:T(8,128)(2,1)S(1)}, bf16[256,1024]{1,0:T(8,128)(2,1)}, u32[]{:S(2)}) copy-start(bf16[256,1024]{1,0:T(8,128)(2,1)} %get-tuple-element.17) | copy-start | bytes 1572868
  204.6 23.7 %copy-start.1 = (bf16[1024,1024]{1,0:T(8,128)(2,1)S(1)}, bf16[1024,1024]{1,0:T(8,128)(2,1)}, u32[]{:S(2)}) copy-start(bf16[1024,1024]{1,0:T(8,128)(2,1)} %param.21) | copy-start | bytes 6291460
Sparse Core Ops, SparseCore 0:
  65.8 53.2 all-gather.6
  120.8 59.7 all-gather.4
where the time goes:
time: 236 us; the launch traced here: 235 us
  blocking collectives  69 us (29%)
  matrix products  46.8 us (20%)
  local copies, waits for them, and re-layouts  44.6 us (19%)
  waiting for transfers between devices  36.7 us (16%)
  between operations  14.4 us (6%)
  other arithmetic  14 us (6%)
  starting transfers between devices  9.7 us (4%)
    all_to_all x1, blocking collectives, per_device(): lax.all_to_all(attended, 'tm', split_axis=0, concat_axis=2, tiled=True)  18.5 us
    all_to_all x1, blocking collectives, per_device(): lax.all_to_all(keys, 'tm', split_axis=2, concat_axis=0, tiled=True)  18.3 us
    all_to_all x1, blocking collectives, per_device(): lax.all_to_all(values, 'tm', split_axis=2, concat_axis=0, tiled=True)  17.9 us
    all_gather x1, waiting for transfers between devices, per_device(): lax.all_gather(values, 'agent', axis=1, tiled=True)  15.4 us
    dot_general x1, matrix products, per_device(): jnp.dot(hidden, w_out, preferred_element_type=jnp.float32)  15 us
    unnamed x1, blocking collectives  14.2 us
    all_gather x1, local copies, waits for them, and re-layouts, per_device(): lax.all_gather(keys, 'agent', axis=1, tiled=True)  12.5 us
    all_gather x1, local copies, waits for them, and re-layouts, per_device(): lax.all_gather(values, 'agent', axis=1, tiled=True)  12.2 us
  transfers between devices with their start and end apart: 4, of which 3 were waited for; matrix products, arithmetic and copies ran while one was open for 22% of the time, Pallas kernels for 0%

commit v1 on v0

--- a/solution.py
+++ b/solution.py
@@ -139,7 +139,10 @@
         jnp.int32(0),
     )
     attended = finish(carry, query.shape)
-    attended = lax.all_to_all(attended, "tm", split_axis=0, concat_axis=2, tiled=True)
+    attended = jnp.concatenate(
+        lax.all_to_all(jnp.stack(jnp.split(attended, lax.axis_size("tm"), axis=0)), "tm", 0, 0),
+        axis=2,
+    )
     projected = jnp.dot(
         attended.reshape(step_count * agent_count, width),
         w_output,

time: 236 us -> 235 us (level)
    unnamed x31 -> x38, local copies, waits for them, and re-layouts: 8.13 us -> 8.15 us
where the time goes in v1:
time: 235 us; the launch traced here: 234 us
  blocking collectives  69.2 us (29%)
  matrix products  46 us (20%)
  local copies, waits for them, and re-layouts  43.9 us (19%)
  waiting for transfers between devices  36.8 us (16%)
  between operations  14.4 us (6%)
  other arithmetic  14.1 us (6%)
  starting transfers between devices  9.71 us (4%)
    all_to_all x1, blocking collectives, per_device(): lax.all_to_all(jnp.stack(jnp.split(attended, lax.axis_size('tm'), axis=0)...  18.6 us
    all_to_all x1, blocking collectives, per_device(): lax.all_to_all(keys, 'tm', split_axis=2, concat_axis=0, tiled=True)  18.3 us
    all_to_all x1, blocking collectives, per_device(): lax.all_to_all(values, 'tm', split_axis=2, concat_axis=0, tiled=True)  17.9 us
    all_gather x1, waiting for transfers between devices, per_device(): lax.all_gather(values, 'agent', axis=1, tiled=True)  15.4 us
    dot_general x1, matrix products, per_device(): jnp.dot(hidden, w_out, preferred_element_type=jnp.float32)  15 us
    unnamed x1, blocking collectives  14.3 us
    all_gather x1, local copies, waits for them, and re-layouts, per_device(): lax.all_gather(keys, 'agent', axis=1, tiled=True)  12.5 us
    all_gather x1, local copies, waits for them, and re-layouts, per_device(): lax.all_gather(values, 'agent', axis=1, tiled=True)  12.2 us
  transfers between devices with their start and end apart: 4, of which 3 were waited for; matrix products, arithmetic and copies ran while one was open for 22% of the time, Pallas kernels for 0%

profile of v1, /device:TPU:0, one launch (start us, length us, event | category | flops | bytes accessed | tf_op | source)
XLA Modules:
  0.0 234.0 jit_solution(10452356320159106458)
XLA Ops:
  6.5 5.3 %collective-permute-start = (bf16[4,64,1024]{2,1,0:T(8,128)(2,1)}, bf16[4,64,1024]{2,1,0:T(8,128)(2,1)S(1)}, u32[]{:S(2)}, u32[]{:S(2)}) collective-permute-start(bf16[4,64,1024]{2,1,0:T(8,128)(2,1)} %param.13), channel_id=1, source_target_pairs={{0,16},{16,32},{32,48},{48,64},{64,80},{80,96},{96,112},{1,17},{17... | collective-permute-start | bytes 1572872 | tf_op jit(solution)/shard_map/ppermute | solution.py:13
  12.8 10.5 %collective-permute-done = bf16[4,64,1024]{2,1,0:T(8,128)(2,1)S(1)} collective-permute-done((bf16[4,64,1024]{2,1,0:T(8,128)(2,1)}, bf16[4,64,1024]{2,1,0:T(8,128)(2,1)S(1)}, u32[]{:S(2)}, u32[]{:S(2)}) %collective-permute-start) | collective-permute-done | bytes 524320 | tf_op jit(solution)/shard_map/ppermute | solution.py:13
  26.9 15.0 %fusion.53 = (f32[256]{0:T(256)S(1)}, bf16[256,1024]{1,0:T(8,128)(2,1)}) fusion(bf16[3072,1024]{1,0:T(8,128)(2,1)} %param.19, bf16[256,1024]{1,0:T(8,128)(2,1)S(1)} %fusion.63, bf16[1024,3072]{1,0:T(8,128)(2,1)} %param.18, bf16[256,1024]{1,0:T(8,128)(2,1)S(1)} %bitcast.74), kind=kOutput, calls=%fused_computation.70 | convolution fusion | flops 3273916160 | bytes 14156800 | tf_op jit(solution)/shard_map/dot_general | solution.py:102
  41.9 1.8 convolution_convert_fusion
  45.4 18.3 %all_to_all.56 = bf16[8,2,16384]{2,1,0:T(2,128)(2,1)S(1)} all-to-all(bf16[8,2,16384]{2,1,0:T(2,128)(2,1)S(1)} %reshape.209), channel_id=1, replica_groups=mesh['tm'=8,'agent'=16] {'tm'}, dimensions={0} | all-to-all | bytes 1048576 | tf_op jit(solution)/shard_map/all_to_all | solution.py:125
  65.8 2.4 %convolution_convert_fusion.2 = bf16[256,1024]{1,0:T(8,128)(2,1)S(1)} fusion(bf16[1024,1024]{1,0:T(8,128)(2,1)} %param.22, bf16[256,1024]{1,0:T(8,128)(2,1)S(1)} %copy-done.8, f32[1024]{0:T(1024)S(1)} %copy-done.5, f32[256]{0:T(256)S(1)} %add_rsqrt_fusion.2), kind=kOutput, calls=%fused_computation.68 | convolution fusion | flops 538181632 | bytes 3150848 | tf_op jit(solution)/shard_map/dot_general | solution.py:118
  69.6 17.9 %all_to_all.57 = bf16[8,2,16384]{2,1,0:T(2,128)(2,1)S(1)} all-to-all(bf16[8,2,16384]{2,1,0:T(2,128)(2,1)S(1)} %reshape.207), channel_id=1, replica_groups=mesh['tm'=8,'agent'=16] {'tm'}, dimensions={0} | all-to-all | bytes 1048576 | tf_op jit(solution)/shard_map/all_to_all | solution.py:126
  88.2 1.4 copy.40
  91.2 14.3 %all-reduce.2 = (s32[1024]{0:T(1024)S(1)}, s32[1024]{0:T(1024)S(1)}) all-reduce(s32[1024]{0:T(1024)S(1)} %dynamic-update-slice, s32[1024]{0:T(1024)S(1)} %dynamic-update-slice.1), channel_id=2, replica_groups=mesh['tm'=8,'agent'=16] {'agent'}, use_global_device_ids=true, to_apply=%add | all-reduce | flops 2048 | bytes 16384
  105.7 2.4 %convolution_convert_fusion.1 = bf16[256,1024]{1,0:T(8,128)(2,1)S(1)} fusion(bf16[1024,1024]{1,0:T(8,128)(2,1)} %param.20, bf16[256,1024]{1,0:T(8,128)(2,1)S(1)} %copy-done.8, f32[1024]{0:T(1024)S(1)} %copy-done.5, f32[256]{0:T(256)S(1)} %add_rsqrt_fusion.2), kind=kOutput, calls=%fused_computation.67 | convolution fusion | flops 538181632 | bytes 3150848 | tf_op jit(solution)/shard_map/dot_general | solution.py:106
  108.9 1.5 reshape.211
  110.4 4.4 %all-to-all-start.1 = ((bf16[8,2,16384]{2,1,0:T(2,128)(2,1)}), bf16[8,2,16384]{2,1,0:T(2,128)(2,1)}, u32[]{:S(2)}, u32[]{:S(2)}) async-start(bf16[8,2,16384]{2,1,0:T(2,128)(2,1)} %reshape.211), calls=%async_computation.1 | async-start | bytes 1048576 | tf_op jit(solution)/shard_map/all_to_all | solution.py:124
  114.8 1.4 and_or_fusion
  116.2 10.9 %all-to-all-done.1 = bf16[8,2,16384]{2,1,0:T(2,128)(2,1)} async-done(((bf16[8,2,16384]{2,1,0:T(2,128)(2,1)}), bf16[8,2,16384]{2,1,0:T(2,128)(2,1)}, u32[]{:S(2)}, u32[]{:S(2)}) %all-to-all-start.1) | async-done | bytes 524320 | tf_op jit(solution)/shard_map/all_to_all | solution.py:124
  127.0 2.7 %reshape.212 = bf16[1024,4,64]{2,1,0:T(4,128)(2,1)S(1)} reshape(bf16[8,2,16384]{2,1,0:T(2,128)(2,1)} %all-to-all-done.1) | data formatting | bytes 1048576
  131.0 2.4 %reshape.187 = bf16[32,64,2,64]{3,2,1,0:T(2,128)(2,1)S(1)} reshape(bf16[8,4,64,128]{3,2,1,0:T(8,128)(2,1)} %bitcast.75) | data formatting | bytes 1048576 | tf_op jit(solution)/shard_map/reshape | solution.py:26
  133.5 12.5 %copy.47 = bf16[32,1024,128]{1,2,0:T(8,128)(2,1)} copy(bf16[32,1024,128]{2,0,1:T(8,128)(2,1)} %all-gather.7.cloned.1.call-done) | data formatting | bytes 16777216 | tf_op jit(solution)/shard_map/all_gather | solution.py:134
  145.9 10.3 %fusion = (f32[32,2,64]{2,1,0:T(2,128)S(1)}, f32[32,2,64,1024]{3,2,1,0:T(8,128)}) fusion(pred[32,64,1024]{2,1,0:T(8,128)(4,1)S(1)} %and_or_fusion, bf16[32,1024,2,64]{1,3,2,0:T(8,128)(2,1)} %bitcast.66, bf16[32,64,2,64]{3,2,1,0:T(2,128)(2,1)S(1)} %reshape.187), kind=kOutput, calls=%fused_computation.3 | convolution fusion | flops 549449728 | bytes 27803648 | tf_op jit(solution)/shard_map/sahd,sbhd->shab/dot_general | solution.py:40
  156.3 9.0 %convert_reduce_fusion = f32[32,2,64]{2,1,0:T(2,128)S(1)} fusion(f32[32,2,64]{2,1,0:T(2,128)S(1)} %broadcast_maximum_fusion, f32[32,2,64,1024]{3,2,1,0:T(8,128)} %get-tuple-element.27, pred[32,64,1024]{2,1,0:T(8,128)(4,1)S(1)} %and_or_fusion), kind=kLoop, calls=%fused_computation | loop fusion | flops 29356032 | bytes 18907136 | tf_op jit(solution)/shard_map/reduce_sum | solution.py:53
  165.3 15.4 %all-gather.5.cloned.1.call-done = bf16[32,1024,128]{2,0,1:T(8,128)(2,1)} async-done(((bf16[32,64,128]{2,0,1:T(8,128)(2,1)}), bf16[32,1024,128]{2,0,1:T(8,128)(2,1)}) %all-gather.5.cloned.1.call-update) | async-done | bytes 8388624 | tf_op jit(solution)/shard_map/all_gather | solution.py:135
  180.7 12.2 %copy.41 = bf16[32,1024,128]{1,2,0:T(8,128)(2,1)} copy(bf16[32,1024,128]{2,0,1:T(8,128)(2,1)} %all-gather.5.cloned.1.call-done) | data formatting | bytes 16777216 | tf_op jit(solution)/shard_map/all_gather | solution.py:135
  192.9 11.0 %fusion.13 = bf16[32,64,2,64]{1,3,2,0:T(8,128)(2,1)S(1)} fusion(bf16[32,1024,2,64]{1,3,2,0:T(8,128)(2,1)} %bitcast.67, f32[32,64,2]{1,2,0:T(2,128)S(1)} %bitcast.91, f32[32,2,64,1024]{3,2,1,0:T(8,128)} %get-tuple-element.27, f32[32,2,64]{2,1,0:T(2,128)S(1)} %broadcast_maximum_fusion, pred[32,64,1024]{2,1,0:T(8,128)(4,1)S(1)} %and_or_fusion), kind=kOutput, calls=%fused_computation.29 | convolution fusion | flops 558366720 | bytes 27820032 | tf_op jit(solution)/shard_map/shab,sbhd->sahd/dot_general | solution.py:54
  205.1 18.6 %all_to_all.58 = bf16[8,4,64,128]{3,2,1,0:T(8,128)(2,1)S(1)} all-to-all(bf16[8,4,64,128]{3,2,1,0:T(8,128)(2,1)S(1)} %constant_dynamic-update-slice_fusion), channel_id=1, replica_groups=mesh['tm'=8,'agent'=16] {'tm'}, dimensions={0} | all-to-all | bytes 1048576 | tf_op jit(solution)/shard_map/all_to_all | solution.py:143
  224.1 3.1 %fusion.49 = bf16[256,1024]{1,0:T(8,128)(2,1)} fusion(bf16[1024,1024]{1,0:T(8,128)(2,1)} %param.23, bf16[256,1024]{1,0:T(8,128)(2,1)S(1)} %copy-done.9, bf16[32,8,8,128]{3,2,1,0:T(8,128)(2,1)S(1)} %bitcast.90), kind=kOutput, calls=%fused_computation.65 | convolution fusion | flops 537657344 | bytes 3670016 | tf_op jit(solution)/shard_map/dot_general | solution.py:146
  (69 shorter events, 14.9 us)
Async XLA Ops:
  6.5 35.4 %copy-start = (bf16[1024,1024]{1,0:T(8,128)(2,1)S(1)}, bf16[1024,1024]{1,0:T(8,128)(2,1)}, u32[]{:S(2)}) copy-start(bf16[1024,1024]{1,0:T(8,128)(2,1)} %param.21) | copy-start | bytes 6291460
  6.5 19.4 %copy-start.2 = (bf16[4,64,1024]{2,1,0:T(8,128)(2,1)S(1)}, bf16[4,64,1024]{2,1,0:T(8,128)(2,1)}, u32[]{:S(2)}) copy-start(bf16[4,64,1024]{2,1,0:T(8,128)(2,1)} %param.13) | copy-start | bytes 1572868
  6.5 126.9 %all-gather.7.cloned.1.call-start = ((), (), s32[]{:S(2)}) async-start(), calls=%async_computation.5 | async-start | bytes 8912896 | tf_op jit(solution)/shard_map/all_gather | solution.py:134
  6.5 16.8 %collective-permute-start = (bf16[4,64,1024]{2,1,0:T(8,128)(2,1)}, bf16[4,64,1024]{2,1,0:T(8,128)(2,1)S(1)}, u32[]{:S(2)}, u32[]{:S(2)}) collective-permute-start(bf16[4,64,1024]{2,1,0:T(8,128)(2,1)} %param.13), channel_id=1, source_target_pairs={{0,16},{16,32},{32,48},{48,64},{64,80},{80,96},{96,112},{1,17},{17... | collective-permute-start | bytes 1572872 | tf_op jit(solution)/shard_map/ppermute | solution.py:13
  26.0 0.7 copy-start.3
  26.9 15.1 %copy-start.5 = (f32[1024]{0:T(1024)S(1)}, f32[1024]{0:T(1024)}, u32[]{:S(2)}) copy-start(f32[1024]{0:T(1024)} %param.17) | copy-start | bytes 12292
  44.6 21.1 %copy-start.8 = (bf16[256,1024]{1,0:T(8,128)(2,1)S(1)}, bf16[256,1024]{1,0:T(8,128)(2,1)}, u32[]{:S(2)}) copy-start(bf16[256,1024]{1,0:T(8,128)(2,1)} %get-tuple-element.25) | copy-start | bytes 1572868
  65.7 115.0 %all-gather.5.cloned.1.call-start = ((), (), s32[]{:S(2)}) async-start(), calls=%async_computation.4 | async-start | bytes 8912896 | tf_op jit(solution)/shard_map/all_gather | solution.py:135
  68.9 20.7 %copy-start.7 = (u32[128]{0:T(128)S(1)}, u32[128]{0:T(128)}, u32[]{:S(2)}) copy-start(u32[128]{0:T(128)} %constant.80) | copy-start | bytes 1540
  68.9 21.9 %copy-start.4 = (s32[64]{0:T(128)S(1)}, s32[64]{0:T(128)}, u32[]{:S(2)}) copy-start(s32[64]{0:T(128)} %param.24) | copy-start | bytes 772
  68.9 22.1 %copy-start.6 = (s32[64]{0:T(128)S(1)}, s32[64]{0:T(128)}, u32[]{:S(2)}) copy-start(s32[64]{0:T(128)} %param.25) | copy-start | bytes 772
  110.4 16.7 %all-to-all-start.1 = ((bf16[8,2,16384]{2,1,0:T(2,128)(2,1)}), bf16[8,2,16384]{2,1,0:T(2,128)(2,1)}, u32[]{:S(2)}, u32[]{:S(2)}) async-start(bf16[8,2,16384]{2,1,0:T(2,128)(2,1)} %reshape.211), calls=%async_computation.1 | async-start | bytes 1048576 | tf_op jit(solution)/shard_map/all_to_all | solution.py:124
  203.9 20.2 %copy-start.9 = (bf16[256,1024]{1,0:T(8,128)(2,1)S(1)}, bf16[256,1024]{1,0:T(8,128)(2,1)}, u32[]{:S(2)}) copy-start(bf16[256,1024]{1,0:T(8,128)(2,1)} %get-tuple-element.25) | copy-start | bytes 1572868
  205.0 22.2 %copy-start.1 = (bf16[1024,1024]{1,0:T(8,128)(2,1)S(1)}, bf16[1024,1024]{1,0:T(8,128)(2,1)}, u32[]{:S(2)}) copy-start(bf16[1024,1024]{1,0:T(8,128)(2,1)} %param.21) | copy-start | bytes 6291460
Sparse Core Ops, SparseCore 0:
  65.8 53.3 all-gather.6
  120.9 59.7 all-gather.4
